TPU v7x, 256 devices: a whole 4x4x8 slice. The times are simulated.
256 devices in a mesh: prow: 8 (over z), pcol: 32 (over x, y, core).
Axes of the slice: x: 4, y: 4, z: 8, core: 2. Of those that a mesh axis runs over, the one named last changes fastest.
Arguments:
- b_panels: bfloat16 [3, 8, 32, 128, 512], P(None, 'prow', 'pcol'), may hold values from -6 to 6
- diag_inverse: bfloat16 [3, 8, 32, 128, 128], P(None, 'prow', 'pcol'), as said below
- l_blocks: bfloat16 [2, 8, 32, 32, 5, 128, 128], P(None, 'prow', 'pcol'), may hold values from -0.0390625 to 0.0390625
- block_cols: int32 [2, 8, 32, 32, 5], P(None, 'prow', 'pcol'), may hold values from 0 to 511, as said below
- live_counts: int32 [2, 8, 32, 32], P(None, 'prow', 'pcol'), may hold values from 0 to 5, as said below
Outputs:
- solution: bfloat16 [3, 8, 32, 128, 512], P(None, 'prow', 'pcol')
Inputs may be any that keep to these rules, and one draw needn't show every extreme that they name: `block_cols`: for block row (l, r, q) and device column c, entries are l2 * 256 + p * 32 + c with l2 < l and 0 <= p < 8; the first live_counts[l - 1, r, c, q] slots are distinct. `live_counts`: at most min(5, l * 8) at level l; that bound is reached at every level. `diag_inverse`: lower triangular.
All inputs are finite; a program needn't handle non-finite values.
Results may differ from a plain program's by a relative error of at most 0.014.
Values may be sent and summed in bfloat16 or wider, within the bound.
A program may use at most 128 MiB of HBM per device.

v0:
```python
import jax
import jax.numpy as jnp
from jax import lax
from jax.sharding import Mesh
from jax.sharding import PartitionSpec as P

PCOL = ("pcol_0", "pcol_1", "pcol_2")


def in_blocks(array, dim, length):
    shape = array.shape
    tiles = array.reshape(*shape[:dim], length, shape[dim] // length, *shape[dim + 1 :])
    return jnp.moveaxis(tiles, dim, 0)


def summed_on_arrival(array, axis, dim):
    tiles = in_blocks(array, dim, lax.axis_size(axis))
    arrived = lax.all_to_all(tiles, axis, split_axis=0, concat_axis=0, tiled=True)
    return arrived.astype(jnp.float32).sum(axis=0)


def summed_rows(array, axes, dim):
    far, near = axes
    tiles = in_blocks(array, dim, lax.axis_size(far))
    nearer = summed_on_arrival(tiles, near, dim + 1)
    arrived = lax.all_to_all(
        nearer.astype(jnp.bfloat16), far, split_axis=0, concat_axis=0, tiled=True
    )
    return arrived.astype(jnp.float32).sum(axis=0)


def from_everyone(array, axis):
    length = lax.axis_size(axis)
    return lax.all_to_all(
        jnp.broadcast_to(array[None], (length, *array.shape)), axis, 0, 0, tiled=True
    )


def joined_along(tiles, dim):
    tiles = jnp.moveaxis(tiles, 0, dim)
    shape = tiles.shape
    return tiles.reshape(*shape[:dim], shape[dim] * shape[dim + 1], *shape[dim + 2 :])


def collect(array, axis, dim):
    tiles = from_everyone(array, axis)
    return joined_along(tiles, dim)


def solve_front(right_cols, diag_inverse, l_blocks, block_cols, live_counts):
    proc_rows = lax.axis_size("prow")
    proc_cols = lax.axis_size(PCOL)
    per_level = proc_rows * proc_cols
    levels = right_cols.shape[0]
    block_size = right_cols.shape[1]
    front_width = right_cols.shape[2]
    slot_count = l_blocks.shape[4]
    solved_cols = jnp.zeros((levels * proc_rows, block_size, front_width), jnp.bfloat16)
    solutions = []
    for level_idx in range(levels):
        right_part = right_cols[level_idx].astype(jnp.float32)
        if level_idx > 0:
            blocks = l_blocks[level_idx - 1, 0, 0]
            chosen = block_cols[level_idx - 1, 0, 0]
            currently_active = live_counts[level_idx - 1, 0, 0]
            local_index = chosen // per_level * proc_rows + chosen % per_level // proc_cols
            known = solved_cols

            def row_term(
                first_row,
                row_count,
                blocks=blocks,
                local_index=local_index,
                currently_active=currently_active,
                known=known,
            ):
                slot_mask = jnp.arange(slot_count)[None, :] < currently_active[:, None]
                masked = jnp.where(slot_mask[:, :, None, None], blocks, jnp.zeros((), jnp.bfloat16))
                fetched = known[local_index]
                return jnp.einsum(
                    "jkab,jkbr->jar", masked, fetched, preferred_element_type=jnp.float32
                )

            row_total = summed_rows(
                row_term(jnp.int32(0), 1 * lax.axis_size(PCOL)).astype(jnp.bfloat16),
                (("pcol_0", "pcol_1"), "pcol_2"),
                0,
            )
            right_part = right_part - row_total[0]
        resid = right_part.astype(jnp.bfloat16)
        solution = jnp.dot(
            diag_inverse[level_idx, 0, 0], resid, preferred_element_type=jnp.float32
        ).astype(jnp.bfloat16)
        solutions.append(solution)
        if level_idx + 1 < levels:
            segment = collect(solution[None], "prow", 0)
            solved_cols = lax.dynamic_update_slice_in_dim(
                solved_cols, segment, level_idx * proc_rows, 0
            )
    return jnp.stack(solutions)


def shards(b_panels, diag_inverse, l_blocks, block_cols, live_counts):
    right_cols = b_panels[:, 0, 0]
    result = solve_front(right_cols, diag_inverse, l_blocks, block_cols, live_counts)
    return result[:, None, None]


def solution(mesh):
    finer = Mesh(
        mesh.devices.reshape(mesh.shape["prow"], 4, 4, 2), ("prow", "pcol_0", "pcol_1", "pcol_2")
    )
    return jax.shard_map(
        shards,
        mesh=finer,
        in_specs=(
            P(None, "prow", PCOL, None, None),
            P(None, "prow", PCOL, None, None),
            P(None, "prow", PCOL, None, None, None, None),
            P(None, "prow", PCOL, None, None),
            P(None, "prow", PCOL, None),
        ),
        out_specs=P(None, "prow", PCOL, None, None),
        check_vma=False,
    )
```

profile of v0, /device:TPU:6, one launch (start us, length us, event | category | flops | bytes accessed | tf_op | source)
XLA Modules:
  0.0 223.2 jit_solution(6519524286480828382)
XLA Ops:
  0.0 1.1 convolution_convert_fusion.2
  1.1 1.1 broadcast_in_dim.40
  2.2 8.5 %all-to-all-start = ((bf16[8,1,128,512]{3,2,1,0:T(8,128)(2,1)}), bf16[8,1,128,512]{3,2,1,0:T(8,128)(2,1)S(1)}, u32[]{:S(2)}, u32[]{:S(2)}) async-start(bf16[8,1,128,512]{3,2,1,0:T(8,128)(2,1)} %broadcast_in_dim.40), calls=%async_computation | async-start | bytes 2097152 | tf_op jit(solution)/shard_map/all_to_all | solution.py:34
  10.6 0.8 compare_select_fusion
  11.4 0.1 copy.25
  11.5 0.1 reshape.406
  11.6 0.7 slice_bitcast_fusion
  12.3 0.1 iota_compare_fusion
  12.4 27.0 %all-to-all-done = bf16[8,1,128,512]{3,2,1,0:T(8,128)(2,1)S(1)} async-done(((bf16[8,1,128,512]{3,2,1,0:T(8,128)(2,1)}), bf16[8,1,128,512]{3,2,1,0:T(8,128)(2,1)S(1)}, u32[]{:S(2)}, u32[]{:S(2)}) %all-to-all-start) | async-done | bytes 1048608 | tf_op jit(solution)/shard_map/all_to_all | solution.py:34
  39.4 0.0 copy-start
  39.4 1.0 copy-done
  40.4 1.5 dynamic_update_slice.6
  41.9 9.5 %gather_fusion = bf16[160,128,512]{2,1,0:T(8,128)(2,1)} fusion(bf16[24,128,512]{2,1,0:T(8,128)(2,1)S(1)} %dynamic_update_slice.6, s32[1024]{0:T(1024)S(1)} %pad_clamp_fusion.1), kind=kCustom, calls=%fused_computation | custom fusion | bytes 41943680 | tf_op jit(solution)/shard_map/gather | solution.py:79
  51.4 14.0 %bitcast_convert_fusion.1 = bf16[32,128,512]{2,1,0:T(8,128)(2,1)} fusion(bf16[32,5,128,512]{3,2,1,0:T(8,128)(2,1)} %bitcast.114, bf16[2,1,1,32,5,128,128]{6,5,4,3,2,1,0:T(8,128)(2,1)} %param.7, pred[32,5]{1,0:T(8,128)(4,1)S(1)} %get-tuple-element.10), kind=kOutput, calls=%fused_computation.3 | convolution fusion | flops 2689073152 | bytes 30408864 | tf_op jit(solution)/shard_map/jkab,jkbr->jar/dot_general | solution.py:80
  65.4 2.6 %copy.40 = bf16[16,2,1,128,512]{4,3,0,2,1:T(8,128)(2,1)S(1)} copy(bf16[16,2,1,128,512]{4,3,1,0,2:T(8,128)(2,1)} %bitcast.120) | data formatting | bytes 8388608 | tf_op jit(solution)/shard_map/reshape;reshape | solution.py:12
  68.1 8.2 %all_to_all.30 = bf16[2,16,1,128,512]{4,3,1,2,0:T(8,128)(2,1)} all-to-all(bf16[2,16,1,128,512]{4,3,1,2,0:T(8,128)(2,1)S(1)} %bitcast.115), channel_id=1, replica_groups=mesh['prow'=8,'pcol_0'=4,'pcol_1'=4,'pcol_2'=2] {'pcol_2'}, dimensions={0} | all-to-all | bytes 8388608 | tf_op jit(solution)/shard_map/all_to_all | solution.py:18
  76.2 0.0 copy-start.1
  76.2 5.0 %reduce_sum.50 = bf16[16,128,512]{2,1,0:T(8,128)(2,1)} reduce(bf16[2,16,1,128,512]{4,3,1,2,0:T(8,128)(2,1)} %all_to_all.30, bf16[]{:T(256)} %constant.60.clone.1), dimensions={0,2}, to_apply=%region_0.1 | reduce | flops 1048576 | bytes 6291458 | tf_op jit(solution)/shard_map/reduce_sum | solution.py:19
  81.2 34.0 %all_to_all.31 = bf16[16,1,128,512]{3,2,1,0:T(8,128)(2,1)S(1)} all-to-all(bf16[16,1,128,512]{3,2,1,0:T(8,128)(2,1)} %bitcast.118), channel_id=1, replica_groups=mesh['prow'=8,'pcol_0'=4,'pcol_1'=4,'pcol_2'=2] {'pcol_0','pcol_1'}, dimensions={0} | all-to-all | bytes 4194304 | tf_op jit(solution)/shard_map/all_to_all | solution.py:26
  115.2 0.3 convert_reduce_fusion.1
  115.5 0.0 copy-done.1
  115.5 1.1 convolution_convert_fusion.1
  116.6 1.1 broadcast_in_dim.42
  117.8 4.2 %all-to-all-start.3 = ((bf16[8,1,128,512]{3,2,1,0:T(8,128)(2,1)}), bf16[8,1,128,512]{3,2,1,0:T(8,128)(2,1)}, u32[]{:S(2)}, u32[]{:S(2)}) async-start(bf16[8,1,128,512]{3,2,1,0:T(8,128)(2,1)} %broadcast_in_dim.42), calls=%async_computation.3 | async-start | bytes 2097152 | tf_op jit(solution)/shard_map/all_to_all | solution.py:34
  122.0 0.1 copy.28
  122.1 0.1 reshape.414
  122.2 27.7 %all-to-all-done.3 = bf16[8,1,128,512]{3,2,1,0:T(8,128)(2,1)} async-done(((bf16[8,1,128,512]{3,2,1,0:T(8,128)(2,1)}), bf16[8,1,128,512]{3,2,1,0:T(8,128)(2,1)}, u32[]{:S(2)}, u32[]{:S(2)}) %all-to-all-start.3) | async-done | bytes 1048608 | tf_op jit(solution)/shard_map/all_to_all | solution.py:34
  149.9 1.3 bitcast_dynamic-update-slice_fusion
  151.2 9.6 %gather_fusion.1 = bf16[160,128,512]{2,1,0:T(8,128)(2,1)} fusion(bf16[24,128,512]{2,1,0:T(8,128)(2,1)S(1)} %bitcast_dynamic-update-slice_fusion, s32[1024]{0:T(1024)S(1)} %pad_clamp_fusion), kind=kCustom, calls=%fused_computation.1 | custom fusion | bytes 41943680 | tf_op jit(solution)/shard_map/gather | solution.py:79
  160.8 14.0 %bitcast_convert_fusion = bf16[32,128,512]{2,1,0:T(8,128)(2,1)} fusion(bf16[32,5,128,512]{3,2,1,0:T(8,128)(2,1)} %bitcast.113, bf16[2,1,1,32,5,128,128]{6,5,4,3,2,1,0:T(8,128)(2,1)} %param.7, pred[32,5]{1,0:T(8,128)(4,1)S(1)} %get-tuple-element.9), kind=kOutput, calls=%fused_computation.2 | convolution fusion | flops 2689073152 | bytes 30408864 | tf_op jit(solution)/shard_map/jkab,jkbr->jar/dot_general | solution.py:80
  174.8 2.6 %copy.39 = bf16[16,2,1,128,512]{4,3,0,2,1:T(8,128)(2,1)S(1)} copy(bf16[16,2,1,128,512]{4,3,1,0,2:T(8,128)(2,1)} %bitcast.121) | data formatting | bytes 8388608 | tf_op jit(solution)/shard_map/reshape;reshape | solution.py:12
  177.5 8.2 %all_to_all.32 = bf16[2,16,1,128,512]{4,3,1,2,0:T(8,128)(2,1)} all-to-all(bf16[2,16,1,128,512]{4,3,1,2,0:T(8,128)(2,1)S(1)} %bitcast.116), channel_id=1, replica_groups=mesh['prow'=8,'pcol_0'=4,'pcol_1'=4,'pcol_2'=2] {'pcol_2'}, dimensions={0} | all-to-all | bytes 8388608 | tf_op jit(solution)/shard_map/all_to_all | solution.py:18
  185.6 3.3 %reduce_sum.54 = bf16[16,128,512]{2,1,0:T(8,128)(2,1)S(1)} reduce(bf16[2,16,1,128,512]{4,3,1,2,0:T(8,128)(2,1)} %all_to_all.32, bf16[]{:T(256)} %constant.60.clone.1), dimensions={0,2}, to_apply=%region_2.3 | reduce | flops 1048576 | bytes 6291458 | tf_op jit(solution)/shard_map/reduce_sum | solution.py:19
  188.9 32.1 %all_to_all.33 = bf16[16,1,128,512]{3,2,1,0:T(8,128)(2,1)S(1)} all-to-all(bf16[16,1,128,512]{3,2,1,0:T(8,128)(2,1)S(1)} %bitcast.117), channel_id=1, replica_groups=mesh['prow'=8,'pcol_0'=4,'pcol_1'=4,'pcol_2'=2] {'pcol_0','pcol_1'}, dimensions={0} | all-to-all | bytes 4194304 | tf_op jit(solution)/shard_map/all_to_all | solution.py:26
  221.0 0.3 convert_reduce_fusion
  221.3 1.1 fusion.8
  222.4 0.8 maximum_bitcast_fusion
  (2 shorter events, 0.0 us)
Async XLA Ops:
  2.2 37.2 %all-to-all-start = ((bf16[8,1,128,512]{3,2,1,0:T(8,128)(2,1)}), bf16[8,1,128,512]{3,2,1,0:T(8,128)(2,1)S(1)}, u32[]{:S(2)}, u32[]{:S(2)}) async-start(bf16[8,1,128,512]{3,2,1,0:T(8,128)(2,1)} %broadcast_in_dim.40), calls=%async_computation | async-start | bytes 2097152 | tf_op jit(solution)/shard_map/all_to_all | solution.py:34
  39.4 1.0 copy-start
  76.2 39.3 %copy-start.1 = (bf16[3,1,1,128,128]{4,3,2,1,0:T(8,128)(2,1)S(1)}, bf16[3,1,1,128,128]{4,3,2,1,0:T(8,128)(2,1)}, u32[]{:S(2)}) copy-start(bf16[3,1,1,128,128]{4,3,2,1,0:T(8,128)(2,1)} %param.6) | copy-start | bytes 294916
  117.8 32.1 %all-to-all-start.3 = ((bf16[8,1,128,512]{3,2,1,0:T(8,128)(2,1)}), bf16[8,1,128,512]{3,2,1,0:T(8,128)(2,1)}, u32[]{:S(2)}, u32[]{:S(2)}) async-start(bf16[8,1,128,512]{3,2,1,0:T(8,128)(2,1)} %broadcast_in_dim.42), calls=%async_computation.3 | async-start | bytes 2097152 | tf_op jit(solution)/shard_map/all_to_all | solution.py:34
where the time goes:
time: 225 us; the launch traced here: 223 us
  blocking collectives  82.5 us (37%)
  waiting for transfers between devices  54.7 us (24%)
  local copies, waits for them, and re-layouts  31.5 us (14%)
  matrix products  31.3 us (14%)
  starting transfers between devices  12.7 us (6%)
  other arithmetic  10.5 us (5%)
    all_to_all x2, blocking collectives, summed_rows(): lax.all_to_all(nearer.astype(jnp.bfloat16), far, split_axis=0, concat_axi...  66.1 us
    all_to_all x2, waiting for transfers between devices, from_everyone(): lax.all_to_all(jnp.broadcast_to(array[None], (length, *array.shape)), axi...  54.7 us
    dot_general x2, matrix products, row_term(): jnp.einsum('jkab,jkbr->jar', masked, fetched, preferred_element_type=jnp....  28 us
    gather x2, local copies, waits for them, and re-layouts, row_term(): fetched = known[local_index]  19.1 us
    all_to_all x2, blocking collectives, summed_on_arrival(): lax.all_to_all(tiles, axis, split_axis=0, concat_axis=0, tiled=True)  16.3 us
    all_to_all x2, starting transfers between devices, from_everyone(): lax.all_to_all(jnp.broadcast_to(array[None], (length, *array.shape)), axi...  12.7 us
    reduce_sum x2, other arithmetic, summed_on_arrival(): return arrived.astype(jnp.float32).sum(axis=0)  8.24 us
    another operation x2, local copies, waits for them, and re-layouts, in_blocks(): array.reshape(*shape[:dim], length, shape[dim] // length, *shape[dim + 1:])  5.27 us
  transfers between devices with their start and end apart: 2, of which 2 were waited for; matrix products, arithmetic and copies ran while one was open for 1% of the time, Pallas kernels for 0%

commit v1 on v0

v1 whole, which is shorter than its diff:
```python
import functools

import jax
import jax.numpy as jnp
from jax import lax
from jax.experimental import pallas as pl
from jax.experimental.pallas import tpu as pltpu
from jax.sharding import Mesh
from jax.sharding import PartitionSpec as P

PCOL = ("pcol_0", "pcol_1", "pcol_2")
CHUNKS = 2
B = 128
RHS = 512
W = RHS // CHUNKS
SLOTS = 5
NZ = 8
HALF = B // 2
QUARTER = B // 4
COPIES = CHUNKS * 2 * (8 + 4 + 12 + 12)
ORDER = ()


def kernel(
    cols, live, b_hbm, d_hbm, l_hbm, out,
    lv, bv, dv, xs, ps, pr, sums, r1, mid, r2, resid,
    in_sem, ssem, rsem, credit,
):
    z = lax.axis_index("prow")
    x = lax.axis_index("pcol_0")
    y = lax.axis_index("pcol_1")
    c = lax.axis_index("pcol_2")
    mate = 1 - c
    away = (("pcol_0", x), ("pcol_1", y))

    def turn(value, step, size):
        return lax.rem(value + (step + size), size)

    loads = {}
    waited = set()

    def load(name, src, dst):
        loads[name] = pltpu.make_async_copy(src, dst, in_sem.at[len(loads)])
        loads[name].start()

    load("d", d_hbm, dv)
    load("b", b_hbm, bv)
    load("l0", l_hbm.at[0], lv.at[0])
    load("l1", l_hbm.at[1], lv.at[1])

    barrier = pltpu.get_barrier_semaphore()
    friends = [{"pcol_2": mate}]
    for axis, value, size in (("pcol_0", x, 4), ("pcol_1", y, 4), ("prow", z, NZ)):
        for step in (1, -1):
            friends.append({axis: turn(value, step, size)})
    for friend in friends:
        pl.semaphore_signal(barrier, inc=1, device_id=friend, device_id_type=pl.DeviceIdType.MESH)

    count = [0]
    started = []

    def send(src, dst, friend):
        at = count[0]
        count[0] += 1
        copy = pltpu.make_async_remote_copy(
            src_ref=src, dst_ref=dst, send_sem=ssem.at[at], recv_sem=rsem.at[at],
            device_id=friend, device_id_type=pl.DeviceIdType.MESH,
        )
        copy.start()
        started.append(copy)
        return copy

    def gather(g, level):
        held = xs[g]
        base = level * NZ
        if level > 0:
            pl.semaphore_wait(credit.at[g, 0], 1)
            pl.semaphore_wait(credit.at[g, 1], 1)
        last = [None, None]
        for step in range(4):
            for d, sign in enumerate((1, -1)):
                if last[d] is not None:
                    last[d].wait_recv()
                slot = held.at[base + turn(z, -sign * step, NZ)]
                if step == 3:
                    slot = slot.at[pl.ds(d * HALF, HALF)]
                last[d] = send(slot, slot, {"prow": turn(z, sign, NZ)})
            yield
        last[0].wait_recv()
        last[1].wait_recv()

    def row_total(g, level, q):
        held = xs[g]
        lefts, rights = [], []
        for k in range(SLOTS):
            v = cols[level, q, k]
            at = (v // 256) * NZ + (v % 256) // 32
            rights.append(held[jnp.where(k < live[level, q], at, 2 * NZ)])
            lefts.append(lv[level, q, k])
        return jnp.dot(
            jnp.concatenate(lefts, axis=1), jnp.concatenate(rights, axis=0),
            preferred_element_type=jnp.float32,
        )

    def products(g, level):
        if level not in waited:
            waited.add(level)
            loads["l%d" % level].wait()
        total = sums.at[level, g]
        pair = [None] * 4
        offsets = (2, 1, -1, 0)
        pending = []

        def theirs(n):
            xd = turn(x, offsets[n], 4)
            for j in range(4):
                q = (xd * 4 + j) * 2 + mate
                ps[level, g, xd, j] = row_total(g, level, q).astype(jnp.bfloat16)
            pair[n] = send(ps.at[level, g, xd], pr.at[level, g, xd], {"pcol_2": mate})

        def ours(n):
            xd = turn(x, offsets[n], 4)
            pair[n].wait_recv()
            for j in range(4):
                q = (xd * 4 + j) * 2 + c
                row = row_total(g, level, q) + pr[level, g, xd, j].astype(jnp.float32)
                total[xd, j] = row.astype(jnp.bfloat16)
        theirs(0)
        for n in range(1, 5):
            if n < 4:
                theirs(n)
            ours(n - 1)
            yield

    def ring(blocks, landing, axis, value, kind, copies, d):
        sign = 1 - 2 * d
        to = {axis: turn(value, sign, 4)}
        if kind == 0:
            src = blocks(turn(value, 2, 4), d)
        elif kind == 1:
            src = blocks(turn(value, sign, 4), 1 - d)
        else:
            copies[d, 0].wait_recv()
            mine = blocks(turn(value, sign, 4), d)
            mine[...] = mine[...] + landing.at[d, 0][...]
            src = mine
        copies[d, kind] = send(src, landing.at[d, kind], to)

    def exchange(g, level):
        total = sums.at[level, g]
        axes = (("pcol_0", x), ("pcol_1", y))

        def first(o):
            def blocks(dest, piece):
                if o == 0:
                    return total.at[dest, pl.ds(2 * piece, 2), pl.ds(0, HALF)]
                return total.at[pl.ds(2 * piece, 2), dest, pl.ds(HALF, HALF)]
            return blocks

        def second(o):
            def blocks(dest, piece):
                return mid.at[level, g, o, dest, pl.ds(QUARTER * piece, QUARTER)]
            return blocks

        one = [{}, {}]
        two = [{}, {}]
        for kind in (0, 1):
            for o in range(2):
                for d in range(2):
                    ring(first(o), r1.at[level, g, o], *axes[o], kind, one[o], d)
        yield
        for o in range(2):
            for d in range(2):
                ring(first(o), r1.at[level, g, o], *axes[o], 2, one[o], d)
        yield
        for o in range(2):
            own = axes[o][1]
            for p in range(2):
                one[o][1 - p, 1].wait_recv()
                one[o][p, 2].wait_recv()
                mine = first(o)(own, p)[...].astype(jnp.float32)
                mine = mine + r1[level, g, o, 1 - p, 1].astype(jnp.float32)
                mine = mine + r1[level, g, o, p, 2].astype(jnp.float32)
                mid[level, g, o, pl.ds(2 * p, 2)] = mine.astype(jnp.bfloat16)
            for kind in (0, 1):
                for d in range(2):
                    ring(second(o), r2.at[level, g, o], *axes[1 - o], kind, two[o], d)
        yield
        for o in range(2):
            for d in range(2):
                ring(second(o), r2.at[level, g, o], *axes[1 - o], 2, two[o], d)
        yield
        for o in range(2):
            own = axes[1 - o][1]
            for p in range(2):
                two[o][1 - p, 1].wait_recv()
                two[o][p, 2].wait_recv()
                mine = second(o)(own, p)[...].astype(jnp.float32)
                mine = mine + r2[level, g, o, 1 - p, 1].astype(jnp.float32)
                mine = mine + r2[level, g, o, p, 2].astype(jnp.float32)
                rows = pl.ds(o * HALF + p * QUARTER, QUARTER)
                right = bv[level + 1, 0, 0, rows, pl.ds(g * W, W)].astype(jnp.float32)
                resid[g, rows] = (right - mine).astype(jnp.bfloat16)

    def solve(g, level, right):
        answer = jnp.dot(
            dv[level, 0, 0], right, preferred_element_type=jnp.float32
        ).astype(jnp.bfloat16)
        out[level, 0, 0, :, pl.ds(g * W, W)] = answer
        if level < 2:
            xs[g][level * NZ + z] = answer

    def chunk(g):
        xs[g][2 * NZ] = jnp.zeros((B, W), jnp.bfloat16)
        solve(g, 0, bv[0, 0, 0, :, pl.ds(g * W, W)])
        if g == 0:
            pl.semaphore_wait(barrier, len(friends))
        for level in range(2):
            yield from gather(g, level)
            yield from products(g, level)
            if level == 0:
                for i, sign in enumerate((1, -1)):
                    pl.semaphore_signal(
                        credit.at[g, i], inc=1, device_id={"prow": turn(z, sign, NZ)},
                        device_id_type=pl.DeviceIdType.MESH,
                    )
            yield from exchange(g, level)
            solve(g, level + 1, resid[g])

    loads["d"].wait()
    loads["b"].wait()
    running = [chunk(g) for g in range(CHUNKS)]
    alive = set(range(CHUNKS))

    def advance(g):
        if g in alive and next(running[g], "end") == "end":
            alive.discard(g)

    for g in ORDER:
        advance(g)
    while alive:
        for g in sorted(alive):
            advance(g)
    for copy in started:
        copy.wait_send()


def shards(b_panels, diag_inverse, l_blocks, block_cols, live_counts):
    any_spec = pl.BlockSpec(memory_space=pl.ANY)
    smem = pl.BlockSpec(memory_space=pltpu.SMEM)
    bf16 = jnp.bfloat16
    return pl.pallas_call(
        kernel,
        name="front",
        out_shape=jax.ShapeDtypeStruct(b_panels.shape, bf16),
        in_specs=[smem, smem, any_spec, any_spec, any_spec],
        out_specs=pl.BlockSpec(memory_space=pltpu.VMEM),
        scratch_shapes=[
            pltpu.VMEM((2, 32, SLOTS, B, B), bf16),
            pltpu.VMEM(b_panels.shape, bf16),
            pltpu.VMEM(diag_inverse.shape, bf16),
            [pltpu.VMEM((2 * NZ + 1, B, W), bf16) for _ in range(CHUNKS)],
            pltpu.VMEM((2, CHUNKS, 4, 4, B, W), bf16),
            pltpu.VMEM((2, CHUNKS, 4, 4, B, W), bf16),
            pltpu.VMEM((2, CHUNKS, 4, 4, B, W), bf16),
            pltpu.VMEM((2, CHUNKS, 2, 2, 3, 2, HALF, W), bf16),
            pltpu.VMEM((2, CHUNKS, 2, 4, HALF, W), bf16),
            pltpu.VMEM((2, CHUNKS, 2, 2, 3, QUARTER, W), bf16),
            pltpu.VMEM((CHUNKS, B, W), bf16),
            pltpu.SemaphoreType.DMA((4,)),
            pltpu.SemaphoreType.DMA((COPIES,)),
            pltpu.SemaphoreType.DMA((COPIES,)),
            pltpu.SemaphoreType.REGULAR((CHUNKS, 2)),
        ],
        compiler_params=pltpu.CompilerParams(
            collective_id=0, has_side_effects=True, vmem_limit_bytes=60 * 2**20
        ),
    )(
        block_cols.reshape(2, 32, SLOTS),
        live_counts.reshape(2, 32),
        b_panels,
        diag_inverse,
        l_blocks.reshape(2, 32, SLOTS, B, B),
    )


def solution(mesh):
    finer = Mesh(
        mesh.devices.reshape(mesh.shape["prow"], 4, 4, 2), ("prow", "pcol_0", "pcol_1", "pcol_2")
    )
    return jax.shard_map(
        shards,
        mesh=finer,
        in_specs=(
            P(None, "prow", PCOL, None, None),
            P(None, "prow", PCOL, None, None),
            P(None, "prow", PCOL, None, None, None, None),
            P(None, "prow", PCOL, None, None),
            P(None, "prow", PCOL, None),
        ),
        out_specs=P(None, "prow", PCOL, None, None),
        check_vma=False,
    )
```

time: 225 us -> 98.1 us (0.44)
  Pallas kernels: 0 us -> 93.6 us
  blocking collectives: 82.5 us -> 0 us
  waiting for transfers between devices: 54.7 us -> 0 us
  matrix products: 31.3 us -> 0 us
  local copies, waits for them, and re-layouts: 31.5 us -> 3.16 us
  starting transfers between devices: 12.7 us -> 0 us
  other arithmetic: 10.5 us -> 0 us
    pallas_call x0 -> x1, Pallas kernels: none -> 93.6 us  [shards(): pl.pallas_call(kernel, name='front', out_shape=jax.ShapeDtypeStruct(b_pan...]
    all_to_all x4 -> x0, blocking collectives: 82.5 us -> none  [the longest x2 66.1 us: summed_rows(): lax.all_to_all(nearer.astype(jnp.bfloat16), far, split_axis=0, concat_axi...]
    all_to_all x2 -> x0, waiting for transfers between devices: 54.7 us -> none  [from_everyone(): lax.all_to_all(jnp.broadcast_to(array[None], (length, *array.shape)), axi...]
    dot_general x5 -> x0, matrix products: 31.3 us -> none  [the longest x2 28 us: row_term(): jnp.einsum('jkab,jkbr->jar', masked, fetched, preferred_element_type=jnp....]
    gather x2 -> x0, local copies, waits for them, and re-layouts: 19.1 us -> none  [row_term(): fetched = known[local_index]]
    all_to_all x2 -> x0, starting transfers between devices: 12.7 us -> none  [from_everyone(): lax.all_to_all(jnp.broadcast_to(array[None], (length, *array.shape)), axi...]
    reduce_sum x4 -> x0, other arithmetic: 8.83 us -> none  [the longest x2 8.24 us: summed_on_arrival(): return arrived.astype(jnp.float32).sum(axis=0)]
    another operation x2 -> x0, local copies, waits for them, and re-layouts: 5.27 us -> none  [in_blocks(): array.reshape(*shape[:dim], length, shape[dim] // length, *shape[dim + 1:])]
  transfers between devices with their start and end apart: 2 -> 0, of which waited for: 2 -> 0; matrix products, arithmetic and copies ran while one was open for 1% -> 0% of each run, Pallas kernels for 0% -> 0%
where the time goes in v1:
time: 98.1 us; the launch traced here: 96.8 us
  Pallas kernels  93.6 us (95%)
  local copies, waits for them, and re-layouts  3.16 us (3%)
    pallas_call x1, Pallas kernels, shards(): pl.pallas_call(kernel, name='front', out_shape=jax.ShapeDtypeStruct(b_pan...  93.6 us
    unnamed x2, local copies, waits for them, and re-layouts  3.16 us

profile of v1, /device:TPU:6, one launch (start us, length us, event | category | flops | bytes accessed | tf_op | source)
XLA Modules:
  0.0 96.8 jit_solution(15982526126657662258)
XLA Ops:
  0.0 1.4 %copy.6 = s32[2,1,1,32,5]{4,3,0,2,1:T(8,128)} copy(s32[2,1,1,32,5]{3,2,4,1,0:T(1,128)} %param.8) | data formatting | bytes 2560 | tf_op args[3]
  1.4 93.6 %front.1 = bf16[3,1,1,128,512]{4,3,2,1,0:T(8,128)(2,1)} custom-call(s32[2,32,5]{2,1,0:T(8,128)} %bitcast.4, s32[2,32]{1,0:T(2,128)} %bitcast.5, bf16[3,1,1,128,512]{4,3,2,1,0:T(8,128)(2,1)} %b_hbm.1, bf16[3,1,1,128,128]{4,3,2,1,0:T(8,128)(2,1)} %d_hbm.1, bf16[2,32,5,128,128]{4,3,2,1,0:T(8,128)(2,1)} %bitcast.3), custom_call_target="tpu_custom_call" | custom-call | tf_op jit(solution)/shard_map/front/pallas_call | solution.py:252
  95.0 1.8 %copy.8 = bf16[3,1,1,128,512]{4,3,2,1,0:T(8,128)(2,1)} copy(bf16[3,1,1,128,512]{4,3,2,1,0:T(8,128)(2,1)} %front.1) | data formatting | bytes 786432

commit v2 on v0

v2 whole, which is shorter than its diff:
```python
import functools

import jax
import jax.numpy as jnp
from jax import lax
from jax.experimental import pallas as pl
from jax.experimental.pallas import tpu as pltpu
from jax.sharding import Mesh
from jax.sharding import PartitionSpec as P

PCOL = ("pcol_0", "pcol_1", "pcol_2")
CHUNKS = 2
B = 128
RHS = 512
W = RHS // CHUNKS
SLOTS = 5
NZ = 8
HALF = B // 2
PIECES = 4
PIECE = B // PIECES
SIGN = (1, -1)
NEAR = (1, 3)
VIA = ((2, 1), (0, 3))
GROUPS = (
    ((2, 2), (2, 0), (0, 2), (2, 1)),
    ((1, 2), (2, 3), (3, 2), (1, 1)),
    ((3, 3), (1, 3), (3, 1), (1, 0)),
    ((0, 1), (3, 0), (0, 3), (0, 0)),
)
ORDER = (
    0, 75, 3, 1, 2, 77, 4, 79, 78, 76, 7, 5, 6, 8, 83, 82, 11, 81, 80, 9, 10, 12, 84, 86, 85,
    87, 13, 14, 15, 16, 17, 18, 19, 88, 20, 31, 21, 89, 22, 29, 24, 23, 30, 32, 92, 90, 91, 33,
    27, 35, 26, 36, 28, 34, 93, 104, 96, 94, 95, 98, 25, 106, 37, 105, 97, 107, 102, 99, 110,
    108, 38, 101, 39, 109, 40, 111, 103, 41, 100, 43, 44, 42, 45, 112, 48, 46, 49, 47, 113, 115,
    116, 114, 50, 51, 117, 52, 120, 118, 119, 53, 54, 55, 121, 124, 56, 122, 123, 58, 66, 57,
    60, 67, 59, 61, 68, 125, 126, 69, 127, 64, 72, 129, 130, 131, 65, 128, 133, 141, 142, 136,
    134, 132, 144, 73, 70, 71, 147, 63, 143, 146, 135, 139, 140, 62, 148, 138, 145, 74, 137,
    149,
)


def goes(step, d):
    if step < 3:
        return tuple(range(PIECES))
    return tuple(h for h in range(PIECES) if h * 2 // PIECES == d)


def plan(g):
    steps = {}
    for lv in range(2):
        after = [] if lv == 0 else [("settle", g, 0, o, r) for o in range(2) for r in range(4)]
        got = [] if lv == 0 else [("two", g, 0, o, r) for o in range(2) for r in (1, 2, 3)]
        sent = [("ag", g, lv, 0, d, h) for h in range(PIECES) for d in range(2)]
        steps["solve", g, lv] = (after, got, sent)
        for step in (1, 2, 3):
            for h in range(PIECES):
                ds = [d for d in range(2) if h in goes(step, d)]
                steps["ag", g, lv, step, h] = (
                    [("solve", g, lv)],
                    [("ag", g, lv, step - 1, d, h) for d in ds],
                    [("ag", g, lv, step, d, h) for d in ds],
                )
        last = [("ag", g, lv, 3, d, h) for d in range(2) for h in goes(3, d)]
        last += [
            ("ag", g, lv, 2, d, h) for d in range(2) for h in range(PIECES) if h not in goes(3, d)
        ]
        for n in range(4):
            before = [("theirs", g, lv, n - 1)] if n else [
                ("ag", g, lv, step, h) for step in (1, 2, 3) for h in range(PIECES)
            ]
            steps["theirs", g, lv, n] = (before, [] if n else last, [("pair", g, lv, n)])
        where = {}
        for n in range(4):
            sent = []
            for row in GROUPS[n]:
                where[row] = n
                for o in range(2):
                    main, r = (row[0], row[1]) if o == 0 else (row[1], row[0])
                    for d in range(2):
                        if main == 2 and r in VIA[d]:
                            sent.append(("far", g, lv, o, d, r))
                        if main == NEAR[d] and r not in VIA[d]:
                            sent.append(("near", g, lv, o, d, r))
            before = [("theirs", g, lv, n)] + ([("ours", g, lv, n - 1)] if n else [])
            steps["ours", g, lv, n] = (before, [("pair", g, lv, n)], sent)
        for o in range(2):
            for d in range(2):
                for r in VIA[d]:
                    row = (NEAR[d], r) if o == 0 else (r, NEAR[d])
                    steps["relay", g, lv, o, d, r] = (
                        [("ours", g, lv, where[row])],
                        [("far", g, lv, o, d, r)],
                        [("near", g, lv, o, d, r)],
                    )
            for r in range(4):
                row = (0, r) if o == 0 else (r, 0)
                steps["settle", g, lv, o, r] = (
                    [("ours", g, lv, where[row])],
                    [("near", g, lv, o, d, r) for d in range(2)],
                    [("two", g, lv, o, r)] if r else [],
                )
    steps["solve", g, 2] = (
        [("settle", g, 1, o, r) for o in range(2) for r in range(4)],
        [("two", g, 1, o, r) for o in range(2) for r in (1, 2, 3)],
        [],
    )
    return steps


def messages():
    return {
        name: at
        for at, name in enumerate(m for g in range(CHUNKS) for s in plan(g).values() for m in s[2])
    }


def kernel(
    cols, live, b_hbm, d_hbm, l_hbm, out,
    lv_ref, bv, dv, xs, ps, pr, sums, far, near, mid, two, resid,
    in_sem, ssem, rsem, credit,
):
    z = lax.axis_index("prow")
    x = lax.axis_index("pcol_0")
    y = lax.axis_index("pcol_1")
    c = lax.axis_index("pcol_2")
    mate = 1 - c
    grid = ("pcol_0", "pcol_1")
    mesh_id = pl.DeviceIdType.MESH

    here = {"prow": z, "pcol_0": x, "pcol_1": y, "pcol_2": c}
    turned = {
        axis: [value] + [lax.rem(value + k, size) for k in range(1, size)]
        for axis, value, size in (("prow", z, NZ), ("pcol_0", x, 4), ("pcol_1", y, 4))
    }

    def turn(axis, step):
        return turned[axis][step % len(turned[axis])]

    def at_device(axis, value):
        return tuple(value if name == axis else here[name] for name in here)

    loads = {}

    def load(name, src, dst):
        loads[name] = pltpu.make_async_copy(src, dst, in_sem.at[len(loads)])
        loads[name].start()

    load("d", d_hbm, dv)
    load("b", b_hbm, bv)
    load("l0", l_hbm.at[0], lv_ref.at[0])
    load("l1", l_hbm.at[1], lv_ref.at[1])

    barrier = pltpu.get_barrier_semaphore()
    friends = [at_device("pcol_2", mate)]
    friends += [at_device(axis, turn(axis, step)) for axis in grid for step in (1, 2, 3)]
    friends += [at_device("prow", turn("prow", sign)) for sign in SIGN]
    for friend in friends:
        pl.semaphore_signal(barrier, inc=1, device_id=friend, device_id_type=mesh_id)

    number = messages()
    copies = {}

    def half(lv, g, o, main, r):
        rx, ry = (main, r) if o == 0 else (r, main)
        return sums.at[lv, g, rx, ry, pl.ds(o * HALF, HALF)]

    def ends(name):
        kind, g, lv = name[:3]
        if kind == "ag":
            step, d, h = name[3:]
            slot = xs[g].at[
                lv * NZ + turn("prow", -SIGN[d] * step), pl.ds(h * PIECE, PIECE)
            ]
            return slot, slot, at_device("prow", turn("prow", SIGN[d]))
        if kind == "pair":
            n = name[3]
            return ps.at[lv, g, n], pr.at[lv, g, n], at_device("pcol_2", mate)
        if kind == "two":
            o, r = name[3:]
            axis = grid[1 - o]
            friend = at_device(axis, turn(axis, r))
            return mid.at[lv, g, o, r], two.at[lv, g, o, r - 1], friend
        o, d, r = name[3:]
        axis = grid[o]
        friend = at_device(axis, turn(axis, SIGN[d]))
        if kind == "far":
            return half(lv, g, o, 2, r), far.at[lv, g, o, d, VIA[d].index(r)], friend
        return half(lv, g, o, NEAR[d], r), near.at[lv, g, o, d, r], friend

    def send(name):
        src, dst, friend = ends(name)
        at = number[name]
        copies[name] = pltpu.make_async_remote_copy(
            src_ref=src, dst_ref=dst, send_sem=ssem.at[at], recv_sem=rsem.at[at],
            device_id=friend, device_id_type=mesh_id,
        )
        copies[name].start()

    def row_total(g, lv, q):
        lefts, rights = [], []
        for k in range(SLOTS):
            v = cols[lv * SLOTS + k, 0, q]
            at = (v >> 8) * NZ + ((v & 255) >> 5)
            rights.append(xs[g][jnp.where(k < live[lv, q], at, 2 * NZ)])
            lefts.append(lv_ref[lv, q, k])
        return jnp.dot(
            jnp.concatenate(lefts, axis=1), jnp.concatenate(rights, axis=0),
            preferred_element_type=jnp.float32,
        )

    def row_of(row, core):
        return (turn("pcol_0", row[0]) * 4 + turn("pcol_1", row[1])) * 2 + core

    def f32(value):
        return value.astype(jnp.float32)

    def do(name):
        kind, g, lv = name[:3]
        if kind == "solve":
            here = pl.ds(g * W, W)
            if lv == 0:
                right = bv[0, 0, 0, :, here]
                xs[g][2 * NZ] = jnp.zeros((B, W), jnp.bfloat16)
            else:
                for o in range(2):
                    total = f32(mid[lv - 1, g, o, 0])
                    for r in range(3):
                        total = total + f32(two[lv - 1, g, o, r])
                    rows = pl.ds(o * HALF, HALF)
                    resid[g, rows] = (f32(bv[lv, 0, 0, rows, here]) - total).astype(jnp.bfloat16)
                right = resid[g]
            answer = jnp.dot(
                dv[lv, 0, 0], right, preferred_element_type=jnp.float32
            ).astype(jnp.bfloat16)
            out[lv, 0, 0, :, here] = answer
            if lv < 2:
                xs[g][lv * NZ + z] = answer
            if lv == 0 and "barrier" not in loads:
                loads["barrier"] = None
                pl.semaphore_wait(barrier, len(friends))
            if lv == 1:
                for i in range(2):
                    pl.semaphore_wait(credit.at[g, i], 1)
        elif kind == "theirs":
            if loads["l%d" % lv] is not None:
                loads["l%d" % lv].wait()
                loads["l%d" % lv] = None
            n = name[3]
            for i, row in enumerate(GROUPS[n]):
                ps[lv, g, n, i] = row_total(g, lv, row_of(row, mate)).astype(jnp.bfloat16)
        elif kind == "ours":
            n = name[3]
            for i, row in enumerate(GROUPS[n]):
                total = row_total(g, lv, row_of(row, c)) + f32(pr[lv, g, n, i])
                sums[lv, g, row[0], row[1]] = total.astype(jnp.bfloat16)
            if n == 3 and lv == 0:
                for i, sign in enumerate(SIGN):
                    pl.semaphore_signal(
                        credit.at[g, i], inc=1, device_id_type=mesh_id,
                        device_id=at_device("prow", turn("prow", sign)),
                    )
        elif kind == "relay":
            o, d, r = name[3:]
            mine = half(lv, g, o, NEAR[d], r)
            mine[...] = mine[...] + far[lv, g, o, d, VIA[d].index(r)]
        elif kind == "settle":
            o, r = name[3:]
            total = f32(half(lv, g, o, 0, r)[...])
            total = total + f32(near[lv, g, o, 0, r]) + f32(near[lv, g, o, 1, r])
            mid[lv, g, o, r] = total.astype(jnp.bfloat16)

    loads["d"].wait()
    loads["b"].wait()
    steps = {}
    for g in range(CHUNKS):
        steps.update(plan(g))
    names = list(steps)
    for at in ORDER:
        name = names[at]
        for message in steps[name][1]:
            copies[message].wait_recv()
        do(name)
        for message in steps[name][2]:
            send(message)
    for copy in copies.values():
        copy.wait_send()


def shards(b_panels, diag_inverse, l_blocks, block_cols, live_counts):
    any_spec = pl.BlockSpec(memory_space=pl.ANY)
    smem = pl.BlockSpec(memory_space=pltpu.SMEM)
    bf16 = jnp.bfloat16
    count = len(messages())
    return pl.pallas_call(
        kernel,
        name="front",
        out_shape=jax.ShapeDtypeStruct(b_panels.shape, bf16),
        in_specs=[smem, smem, any_spec, any_spec, any_spec],
        out_specs=pl.BlockSpec(memory_space=pltpu.VMEM),
        scratch_shapes=[
            pltpu.VMEM((2, 32, SLOTS, B, B), bf16),
            pltpu.VMEM(b_panels.shape, bf16),
            pltpu.VMEM(diag_inverse.shape, bf16),
            [pltpu.VMEM((2 * NZ + 1, B, W), bf16) for _ in range(CHUNKS)],
            pltpu.VMEM((2, CHUNKS, 4, 4, B, W), bf16),
            pltpu.VMEM((2, CHUNKS, 4, 4, B, W), bf16),
            pltpu.VMEM((2, CHUNKS, 4, 4, B, W), bf16),
            pltpu.VMEM((2, CHUNKS, 2, 2, 2, HALF, W), bf16),
            pltpu.VMEM((2, CHUNKS, 2, 2, 4, HALF, W), bf16),
            pltpu.VMEM((2, CHUNKS, 2, 4, HALF, W), bf16),
            pltpu.VMEM((2, CHUNKS, 2, 3, HALF, W), bf16),
            pltpu.VMEM((CHUNKS, B, W), bf16),
            pltpu.SemaphoreType.DMA((4,)),
            pltpu.SemaphoreType.DMA((count,)),
            pltpu.SemaphoreType.DMA((count,)),
            pltpu.SemaphoreType.REGULAR((CHUNKS, 2)),
        ],
        compiler_params=pltpu.CompilerParams(
            collective_id=0, has_side_effects=True, vmem_limit_bytes=60 * 2**20
        ),
    )(
        block_cols.transpose(0, 1, 4, 2, 3).reshape(2 * SLOTS, 1, 32),
        live_counts.reshape(2, 32),
        b_panels,
        diag_inverse,
        l_blocks.reshape(2, 32, SLOTS, B, B),
    )


def solution(mesh):
    finer = Mesh(
        mesh.devices.reshape(mesh.shape["prow"], 4, 4, 2), ("prow", "pcol_0", "pcol_1", "pcol_2")
    )
    return jax.shard_map(
        shards,
        mesh=finer,
        in_specs=(
            P(None, "prow", PCOL, None, None),
            P(None, "prow", PCOL, None, None),
            P(None, "prow", PCOL, None, None, None, None),
            P(None, "prow", PCOL, None, None),
            P(None, "prow", PCOL, None),
        ),
        out_specs=P(None, "prow", PCOL, None, None),
        check_vma=False,
    )
```

time: 225 us -> 83.2 us (0.37)
  blocking collectives: 82.5 us -> 0 us
  Pallas kernels: 0 us -> 80 us
  waiting for transfers between devices: 54.7 us -> 0 us
  matrix products: 31.3 us -> 0 us
  local copies, waits for them, and re-layouts: 31.5 us -> 1.77 us
  starting transfers between devices: 12.7 us -> 0 us
  other arithmetic: 10.5 us -> 0 us
    all_to_all x4 -> x0, blocking collectives: 82.5 us -> none  [the longest x2 66.1 us: summed_rows(): lax.all_to_all(nearer.astype(jnp.bfloat16), far, split_axis=0, concat_axi...]
    pallas_call x0 -> x1, Pallas kernels: none -> 80 us  [shards(): pl.pallas_call(kernel, name='front', out_shape=jax.ShapeDtypeStruct(b_pan...]
    all_to_all x2 -> x0, waiting for transfers between devices: 54.7 us -> none  [from_everyone(): lax.all_to_all(jnp.broadcast_to(array[None], (length, *array.shape)), axi...]
    dot_general x5 -> x0, matrix products: 31.3 us -> none  [the longest x2 28 us: row_term(): jnp.einsum('jkab,jkbr->jar', masked, fetched, preferred_element_type=jnp....]
    gather x2 -> x0, local copies, waits for them, and re-layouts: 19.1 us -> none  [row_term(): fetched = known[local_index]]
    all_to_all x2 -> x0, starting transfers between devices: 12.7 us -> none  [from_everyone(): lax.all_to_all(jnp.broadcast_to(array[None], (length, *array.shape)), axi...]
    reduce_sum x4 -> x0, other arithmetic: 8.83 us -> none  [the longest x2 8.24 us: summed_on_arrival(): return arrived.astype(jnp.float32).sum(axis=0)]
    another operation x2 -> x0, local copies, waits for them, and re-layouts: 5.27 us -> none  [in_blocks(): array.reshape(*shape[:dim], length, shape[dim] // length, *shape[dim + 1:])]
  transfers between devices with their start and end apart: 2 -> 0, of which waited for: 2 -> 0; matrix products, arithmetic and copies ran while one was open for 1% -> 0% of each run, Pallas kernels for 0% -> 0%
where the time goes in v2:
time: 83.2 us; the launch traced here: 81.8 us
  Pallas kernels  80 us (96%)
  local copies, waits for them, and re-layouts  1.77 us (2%)
    pallas_call x1, Pallas kernels, shards(): pl.pallas_call(kernel, name='front', out_shape=jax.ShapeDtypeStruct(b_pan...  80 us
    unnamed x1, local copies, waits for them, and re-layouts  1.77 us

profile of v2, /device:TPU:6, one launch (start us, length us, event | category | flops | bytes accessed | tf_op | source)
XLA Modules:
  0.0 81.8 jit_solution(9477668712988931264)
XLA Ops:
  0.0 80.0 %front.1 = bf16[3,1,1,128,512]{4,3,2,1,0:T(8,128)(2,1)} custom-call(s32[10,1,32]{2,1,0:T(1,128)} %bitcast.6, s32[2,32]{1,0:T(2,128)} %bitcast.7, bf16[3,1,1,128,512]{4,3,2,1,0:T(8,128)(2,1)} %b_hbm.1, bf16[3,1,1,128,128]{4,3,2,1,0:T(8,128)(2,1)} %d_hbm.1, bf16[2,32,5,128,128]{4,3,2,1,0:T(8,128)(2,1)} %bitcast.5), custom_call_target="tpu_custom_call" | custom-call | tf_op jit(solution)/shard_map/front/pallas_call | solution.py:294
  80.0 1.8 %copy.7 = bf16[3,1,1,128,512]{4,3,2,1,0:T(8,128)(2,1)} copy(bf16[3,1,1,128,512]{4,3,2,1,0:T(8,128)(2,1)} %front.1) | data formatting | bytes 786432

commit v3 on v2

--- a/solution.py
+++ b/solution.py
@@ -16,7 +16,7 @@
 SLOTS = 5
 NZ = 8
 HALF = B // 2
-PIECES = 4
+PIECES = 2
 PIECE = B // PIECES
 SIGN = (1, -1)
 NEAR = (1, 3)
@@ -28,14 +28,13 @@
     ((0, 1), (3, 0), (0, 3), (0, 0)),
 )
 ORDER = (
-    0, 75, 3, 1, 2, 77, 4, 79, 78, 76, 7, 5, 6, 8, 83, 82, 11, 81, 80, 9, 10, 12, 84, 86, 85,
-    87, 13, 14, 15, 16, 17, 18, 19, 88, 20, 31, 21, 89, 22, 29, 24, 23, 30, 32, 92, 90, 91, 33,
-    27, 35, 26, 36, 28, 34, 93, 104, 96, 94, 95, 98, 25, 106, 37, 105, 97, 107, 102, 99, 110,
-    108, 38, 101, 39, 109, 40, 111, 103, 41, 100, 43, 44, 42, 45, 112, 48, 46, 49, 47, 113, 115,
-    116, 114, 50, 51, 117, 52, 120, 118, 119, 53, 54, 55, 121, 124, 56, 122, 123, 58, 66, 57,
-    60, 67, 59, 61, 68, 125, 126, 69, 127, 64, 72, 129, 130, 131, 65, 128, 133, 141, 142, 136,
-    134, 132, 144, 73, 70, 71, 147, 63, 143, 146, 135, 139, 140, 62, 148, 138, 145, 74, 137,
-    149,
+    0, 71, 2, 1, 4, 3, 73, 72, 75, 74, 6, 5, 8, 7, 77, 76, 79, 78, 9, 10, 80, 81, 11, 12, 13,
+    82, 83, 84, 15, 16, 86, 87, 19, 17, 20, 27, 14, 90, 28, 22, 30, 88, 98, 85, 91, 99, 93, 101,
+    25, 33, 18, 29, 21, 24, 32, 26, 34, 96, 104, 89, 92, 100, 103, 95, 97, 105, 23, 31, 35, 94,
+    102, 106, 37, 36, 39, 38, 108, 107, 110, 109, 41, 40, 43, 42, 112, 111, 114, 113, 44, 45,
+    115, 116, 46, 47, 48, 117, 118, 50, 51, 121, 122, 119, 62, 54, 52, 49, 55, 63, 57, 65, 133,
+    125, 120, 123, 128, 126, 60, 68, 53, 136, 56, 64, 134, 67, 59, 61, 69, 131, 139, 124, 127,
+    135, 130, 138, 132, 140, 58, 66, 70, 129, 137, 141,
 )
 
 
@@ -54,19 +53,22 @@
         steps["solve", g, lv] = (after, got, sent)
         for step in (1, 2, 3):
             for h in range(PIECES):
-                ds = [d for d in range(2) if h in goes(step, d)]
-                steps["ag", g, lv, step, h] = (
-                    [("solve", g, lv)],
-                    [("ag", g, lv, step - 1, d, h) for d in ds],
-                    [("ag", g, lv, step, d, h) for d in ds],
-                )
+                for d in range(2):
+                    if h in goes(step, d):
+                        steps["ag", g, lv, step, d, h] = (
+                            [("ag", g, lv, step, d, h - 1) if h - 1 in goes(step, d)
+                             else ("solve", g, lv)],
+                            [("ag", g, lv, step - 1, d, h)],
+                            [("ag", g, lv, step, d, h)],
+                        )
         last = [("ag", g, lv, 3, d, h) for d in range(2) for h in goes(3, d)]
         last += [
             ("ag", g, lv, 2, d, h) for d in range(2) for h in range(PIECES) if h not in goes(3, d)
         ]
         for n in range(4):
             before = [("theirs", g, lv, n - 1)] if n else [
-                ("ag", g, lv, step, h) for step in (1, 2, 3) for h in range(PIECES)
+                ("ag", g, lv, step, d, h)
+                for step in (1, 2, 3) for d in range(2) for h in goes(step, d)
             ]
             steps["theirs", g, lv, n] = (before, [] if n else last, [("pair", g, lv, n)])
         where = {}
@@ -115,9 +117,9 @@
 
 
 def kernel(
-    cols, live, b_hbm, d_hbm, l_hbm, out,
-    lv_ref, bv, dv, xs, ps, pr, sums, far, near, mid, two, resid,
-    in_sem, ssem, rsem, credit,
+    cols_hbm, live_hbm, b_hbm, d_hbm, l_hbm, out_hbm,
+    cols, live, out, lv_ref, bv, dv, xs, ps, pr, sums, far, near, mid, two, resid,
+    in_sem, out_sem, ssem, rsem, credit,
 ):
     z = lax.axis_index("prow")
     x = lax.axis_index("pcol_0")
@@ -146,8 +148,12 @@
         loads[name].start()
 
     load("d", d_hbm, dv)
-    load("b", b_hbm, bv)
+    load("b0", b_hbm.at[0], bv.at[0])
+    load("cols", cols_hbm, cols)
+    load("live", live_hbm, live)
     load("l0", l_hbm.at[0], lv_ref.at[0])
+    load("b1", b_hbm.at[1], bv.at[1])
+    load("b2", b_hbm.at[2], bv.at[2])
     load("l1", l_hbm.at[1], lv_ref.at[1])
 
     barrier = pltpu.get_barrier_semaphore()
@@ -159,6 +165,7 @@
 
     number = messages()
     copies = {}
+    stored, writes = [], []
 
     def half(lv, g, o, main, r):
         rx, ry = (main, r) if o == 0 else (r, main)
@@ -214,6 +221,11 @@
     def f32(value):
         return value.astype(jnp.float32)
 
+    def need_load(name):
+        if loads[name] is not None:
+            loads[name].wait()
+            loads[name] = None
+
     def do(name):
         kind, g, lv = name[:3]
         if kind == "solve":
@@ -222,6 +234,7 @@
                 right = bv[0, 0, 0, :, here]
                 xs[g][2 * NZ] = jnp.zeros((B, W), jnp.bfloat16)
             else:
+                need_load("b%d" % lv)
                 for o in range(2):
                     total = f32(mid[lv - 1, g, o, 0])
                     for r in range(3):
@@ -233,6 +246,10 @@
                 dv[lv, 0, 0], right, preferred_element_type=jnp.float32
             ).astype(jnp.bfloat16)
             out[lv, 0, 0, :, here] = answer
+            stored.append(lv)
+            if stored.count(lv) == CHUNKS:
+                writes.append(pltpu.make_async_copy(out.at[lv], out_hbm.at[lv], out_sem.at[lv]))
+                writes[-1].start()
             if lv < 2:
                 xs[g][lv * NZ + z] = answer
             if lv == 0 and "barrier" not in loads:
@@ -242,9 +259,8 @@
                 for i in range(2):
                     pl.semaphore_wait(credit.at[g, i], 1)
         elif kind == "theirs":
-            if loads["l%d" % lv] is not None:
-                loads["l%d" % lv].wait()
-                loads["l%d" % lv] = None
+            for need in ("cols", "live", "l%d" % lv):
+                need_load(need)
             n = name[3]
             for i, row in enumerate(GROUPS[n]):
                 ps[lv, g, n, i] = row_total(g, lv, row_of(row, mate)).astype(jnp.bfloat16)
@@ -270,7 +286,7 @@
             mid[lv, g, o, r] = total.astype(jnp.bfloat16)
 
     loads["d"].wait()
-    loads["b"].wait()
+    loads["b0"].wait()
     steps = {}
     for g in range(CHUNKS):
         steps.update(plan(g))
@@ -284,20 +300,24 @@
             send(message)
     for copy in copies.values():
         copy.wait_send()
+    for write in writes:
+        write.wait()
 
 
 def shards(b_panels, diag_inverse, l_blocks, block_cols, live_counts):
     any_spec = pl.BlockSpec(memory_space=pl.ANY)
-    smem = pl.BlockSpec(memory_space=pltpu.SMEM)
     bf16 = jnp.bfloat16
     count = len(messages())
     return pl.pallas_call(
         kernel,
         name="front",
         out_shape=jax.ShapeDtypeStruct(b_panels.shape, bf16),
-        in_specs=[smem, smem, any_spec, any_spec, any_spec],
-        out_specs=pl.BlockSpec(memory_space=pltpu.VMEM),
+        in_specs=[any_spec] * 5,
+        out_specs=any_spec,
         scratch_shapes=[
+            pltpu.SMEM((2 * SLOTS, 1, 32), jnp.int32),
+            pltpu.SMEM((2, 32), jnp.int32),
+            pltpu.VMEM(b_panels.shape, bf16),
             pltpu.VMEM((2, 32, SLOTS, B, B), bf16),
             pltpu.VMEM(b_panels.shape, bf16),
             pltpu.VMEM(diag_inverse.shape, bf16),
@@ -310,7 +330,8 @@
             pltpu.VMEM((2, CHUNKS, 2, 4, HALF, W), bf16),
             pltpu.VMEM((2, CHUNKS, 2, 3, HALF, W), bf16),
             pltpu.VMEM((CHUNKS, B, W), bf16),
-            pltpu.SemaphoreType.DMA((4,)),
+            pltpu.SemaphoreType.DMA((8,)),
+            pltpu.SemaphoreType.DMA((3,)),
             pltpu.SemaphoreType.DMA((count,)),
             pltpu.SemaphoreType.DMA((count,)),
             pltpu.SemaphoreType.REGULAR((CHUNKS, 2)),

time: 83.2 us -> 76.7 us (0.922)
  Pallas kernels: 80 us -> 74.1 us
    pallas_call x1, Pallas kernels: 80 us -> 74.1 us  [shards(): pl.pallas_call(kernel, name='front', out_shape=jax.ShapeDtypeStruct(b_pan...]
where the time goes in v3:
time: 76.7 us; the launch traced here: 75.8 us
  Pallas kernels  74.1 us (97%)
  local copies, waits for them, and re-layouts  1.77 us (2%)
    pallas_call x1, Pallas kernels, shards(): pl.pallas_call(kernel, name='front', out_shape=jax.ShapeDtypeStruct(b_pan...  74.1 us
    unnamed x1, local copies, waits for them, and re-layouts  1.77 us

profile of v3, /device:TPU:6, one launch (start us, length us, event | category | flops | bytes accessed | tf_op | source)
XLA Modules:
  0.0 75.8 jit_solution(5458180297379517632)
XLA Ops:
  0.0 74.1 %front.1 = bf16[3,1,1,128,512]{4,3,2,1,0:T(8,128)(2,1)} custom-call(s32[10,1,32]{2,1,0:T(1,128)} %bitcast.6, s32[2,32]{1,0:T(2,128)} %bitcast.7, bf16[3,1,1,128,512]{4,3,2,1,0:T(8,128)(2,1)} %b_hbm.1, bf16[3,1,1,128,128]{4,3,2,1,0:T(8,128)(2,1)} %d_hbm.1, bf16[2,32,5,128,128]{4,3,2,1,0:T(8,128)(2,1)} %bitcast.5), custom_call_target="tpu_custom_call" | custom-call | tf_op jit(solution)/shard_map/front/pallas_call | solution.py:311
  74.1 1.8 %copy.7 = bf16[3,1,1,128,512]{4,3,2,1,0:T(8,128)(2,1)} copy(bf16[3,1,1,128,512]{4,3,2,1,0:T(8,128)(2,1)} %front.1) | data formatting | bytes 786432

commit v4 on v3

--- a/solution.py
+++ b/solution.py
@@ -29,12 +29,12 @@
 )
 ORDER = (
     0, 71, 2, 1, 4, 3, 73, 72, 75, 74, 6, 5, 8, 7, 77, 76, 79, 78, 9, 10, 80, 81, 11, 12, 13,
-    82, 83, 84, 15, 16, 86, 87, 19, 17, 20, 27, 14, 90, 28, 22, 30, 88, 98, 85, 91, 99, 93, 101,
-    25, 33, 18, 29, 21, 24, 32, 26, 34, 96, 104, 89, 92, 100, 103, 95, 97, 105, 23, 31, 35, 94,
+    82, 83, 15, 16, 86, 87, 84, 17, 27, 19, 14, 20, 28, 22, 30, 88, 98, 90, 85, 91, 99, 93, 101,
+    25, 33, 18, 21, 29, 32, 24, 26, 34, 104, 96, 89, 92, 100, 103, 95, 97, 105, 23, 31, 35, 94,
     102, 106, 37, 36, 39, 38, 108, 107, 110, 109, 41, 40, 43, 42, 112, 111, 114, 113, 44, 45,
-    115, 116, 46, 47, 48, 117, 118, 50, 51, 121, 122, 119, 62, 54, 52, 49, 55, 63, 57, 65, 133,
-    125, 120, 123, 128, 126, 60, 68, 53, 136, 56, 64, 134, 67, 59, 61, 69, 131, 139, 124, 127,
-    135, 130, 138, 132, 140, 58, 66, 70, 129, 137, 141,
+    115, 116, 46, 47, 48, 117, 118, 50, 51, 121, 122, 119, 62, 52, 54, 49, 55, 63, 57, 65, 133,
+    125, 123, 120, 126, 134, 128, 136, 60, 68, 53, 56, 64, 67, 59, 61, 69, 131, 139, 124, 127,
+    135, 138, 130, 132, 140, 58, 66, 70, 129, 137, 141,
 )
 
 

time: 76.7 us -> 76.2 us (level); the launches traced: 75.8 us -> 76.1 us
  no operation moved by 1% of the time
where the time goes in v4:
time: 76.2 us; the launch traced here: 76.1 us
  Pallas kernels  74.3 us (98%)
  local copies, waits for them, and re-layouts  1.77 us (2%)
    pallas_call x1, Pallas kernels, shards(): pl.pallas_call(kernel, name='front', out_shape=jax.ShapeDtypeStruct(b_pan...  74.3 us
    unnamed x1, local copies, waits for them, and re-layouts  1.77 us

profile of v4, /device:TPU:6, one launch (start us, length us, event | category | flops | bytes accessed | tf_op | source)
XLA Modules:
  0.0 76.1 jit_solution(494436933362838313)
XLA Ops:
  0.0 74.3 %front.1 = bf16[3,1,1,128,512]{4,3,2,1,0:T(8,128)(2,1)} custom-call(s32[10,1,32]{2,1,0:T(1,128)} %bitcast.6, s32[2,32]{1,0:T(2,128)} %bitcast.7, bf16[3,1,1,128,512]{4,3,2,1,0:T(8,128)(2,1)} %b_hbm.1, bf16[3,1,1,128,128]{4,3,2,1,0:T(8,128)(2,1)} %d_hbm.1, bf16[2,32,5,128,128]{4,3,2,1,0:T(8,128)(2,1)} %bitcast.5), custom_call_target="tpu_custom_call" | custom-call | tf_op jit(solution)/shard_map/front/pallas_call | solution.py:311
  74.3 1.8 %copy.7 = bf16[3,1,1,128,512]{4,3,2,1,0:T(8,128)(2,1)} copy(bf16[3,1,1,128,512]{4,3,2,1,0:T(8,128)(2,1)} %front.1) | data formatting | bytes 786432
